TPU v7x, 32 devices: a whole 2x2x4 slice. The times are simulated.
32 devices in a mesh: seq: 8 (over y, x, core), chan: 4 (over z).
Axes of the slice: x: 2, y: 2, z: 4, core: 2. Of those that a mesh axis runs over, the one named last changes fastest.
Arguments:
- hidden_states: bfloat16 [4096, 2048], P('chan', 'seq'), may hold values from -700 to 700
- norm_gain: float32 [4096], P('chan'), may hold values from 0.1 to 1.9
- short_filter: float32 [4096, 128], P('chan'), may hold values from -0.5 to 0.5
- long_filter: bfloat16 [4096, 2048], P('chan', 'seq'), may hold values from -0.125 to 0.125
- long_bias: float32 [4096], P('chan'), may hold values from -4 to 4
- gate_stream: bfloat16 [4096, 2048], P('chan', 'seq'), may hold values from -6 to 6
- upstream: bfloat16 [4096, 2048], P(None, 'seq'), may hold values from -6 to 6
Outputs:
- mixed: bfloat16 [4096, 2048], P('chan', 'seq')
- weight_grad: float32 [4096, 4096], P('seq', 'chan')
All inputs are finite; a program needn't handle non-finite values.
Results may differ from a plain program's by a relative error of at most 0.015.
Values may be sent and summed in bfloat16 or wider, within the bound.
A program may use at most 64 MiB of HBM per device.

v0:
```python
import math

import jax
import jax.numpy as jnp
from jax import lax
from jax.sharding import PartitionSpec as P

D = 4096


EPSILON = 1e-05


def passed_along(value, axis, by):
    devices = lax.axis_size(axis)
    pairs = [(i, i + by) for i in range(devices) if 0 <= i + by < devices]
    return lax.ppermute(value, axis, pairs)


def short_conv(padded, taps):
    kernel = taps[:, ::-1][:, None, :]
    result = lax.conv_general_dilated(
        padded[None],
        kernel,
        (1,),
        "VALID",
        dimension_numbers=("NCH", "OIH", "NCH"),
        feature_group_count=padded.shape[0],
        precision=lax.Precision.HIGHEST,
    )
    return result[0]


def twiddle(row_total, col_total, modulus, direction):
    product = (
        jnp.arange(row_total, dtype=jnp.int32)[:, None]
        * jnp.arange(col_total, dtype=jnp.int32)[None, :]
        % modulus
    )
    angles = direction * 2.0 * math.pi * product.astype(jnp.float32) / modulus
    return (jnp.cos(angles), jnp.sin(angles))


def product_einsum(form, left, right):
    return jnp.einsum(form, left, right, precision=lax.Precision.HIGHEST)


def split_table(table):
    upper = table.astype(jnp.bfloat16)
    lower = (table - upper.astype(jnp.float32)).astype(jnp.bfloat16)
    return (upper, lower)


def table_product(table, grid):
    upper, lower = split_table(table)
    first = jnp.einsum("kn,cnm->ckm", upper, grid, preferred_element_type=jnp.float32)
    return first + jnp.einsum("kn,cnm->ckm", lower, grid, preferred_element_type=jnp.float32)


def forward_real(signal, factor_a, factor_b):
    length = factor_a * factor_b
    seq_total = signal.shape[1]
    kept_in = -(-seq_total // factor_b)
    filled = jnp.pad(signal, ((0, 0), (0, kept_in * factor_b - seq_total)))
    grid = filled.reshape(signal.shape[0], kept_in, factor_b)
    outer_re, outer_im = twiddle(factor_a, kept_in, factor_a, -1.0)
    section_re = table_product(outer_re, grid)
    section_im = table_product(outer_im, grid)
    turn_re, turn_im = twiddle(factor_a, factor_b, length, -1.0)
    rotated_re = section_re * turn_re - section_im * turn_im
    rotated_im = section_re * turn_im + section_im * turn_re
    inner_re, inner_im = twiddle(factor_b, factor_b, factor_b, -1.0)
    result_re = product_einsum("ckm,jm->ckj", rotated_re, inner_re) - product_einsum(
        "ckm,jm->ckj", rotated_im, inner_im
    )
    result_im = product_einsum("ckm,jm->ckj", rotated_re, inner_im) + product_einsum(
        "ckm,jm->ckj", rotated_im, inner_re
    )
    return (result_re, result_im)


def inverse_real(spec_re, spec_im, factor_a, factor_b, kept_rows):
    length = factor_a * factor_b
    inner_re, inner_im = twiddle(factor_b, factor_b, factor_b, 1.0)
    section_re = product_einsum("ckj,mj->ckm", spec_re, inner_re) - product_einsum(
        "ckj,mj->ckm", spec_im, inner_im
    )
    section_im = product_einsum("ckj,mj->ckm", spec_re, inner_im) + product_einsum(
        "ckj,mj->ckm", spec_im, inner_re
    )
    turn_re, turn_im = twiddle(factor_a, factor_b, length, 1.0)
    rotated_re = section_re * turn_re - section_im * turn_im
    rotated_im = section_re * turn_im + section_im * turn_re
    outer_re, outer_im = twiddle(kept_rows, factor_a, factor_a, 1.0)
    result = product_einsum("nk,ckm->cnm", outer_re, rotated_re) - product_einsum(
        "nk,ckm->cnm", outer_im, rotated_im
    )
    return result.reshape(result.shape[0], kept_rows * factor_b) / length


def long_convolution(signal, filt):
    seq_total = signal.shape[1]
    length = 2 * seq_total
    factor_a = 1
    for divisor in range(1, math.isqrt(length) + 1):
        if length % divisor == 0:
            factor_a = divisor
    factor_b = length // factor_a
    signal_re, signal_im = forward_real(signal, factor_a, factor_b)
    filter_re, filter_im = forward_real(filt, factor_a, factor_b)
    joint_re = signal_re * filter_re - signal_im * filter_im
    joint_im = signal_re * filter_im + signal_im * filter_re
    kept_rows = -(-seq_total // factor_b)
    return inverse_real(joint_re, joint_im, factor_a, factor_b, kept_rows)[:, :seq_total]


def shards(hidden_states, norm_gain, short_filter, long_filter, long_bias, gate_stream, upstream):
    states = hidden_states.astype(jnp.float32)
    partial_squares = jnp.sum(states * states, axis=0)
    squares = lax.psum(partial_squares, "chan")
    normed = (states * lax.rsqrt(squares / D + EPSILON)[None, :] * norm_gain[:, None]).astype(
        jnp.bfloat16
    )
    tap_count = short_filter.shape[1]
    width_local = hidden_states.shape[0] // lax.axis_size("seq")
    owner_index = lax.axis_index("seq")
    bias_slice = lax.dynamic_slice_in_dim(long_bias, owner_index * width_local, width_local)
    tail_cols = normed[:, normed.shape[1] - tap_count :]
    from_left = passed_along(tail_cols, "seq", 1)
    padded = jnp.concatenate(
        [from_left[:, 1:].astype(jnp.float32), normed.astype(jnp.float32)], axis=1
    )
    short_out = short_conv(padded, short_filter).astype(jnp.bfloat16)
    short_whole, filter_whole = (
        lax.all_to_all(short_out, "seq", split_axis=0, concat_axis=1, tiled=True),
        lax.all_to_all(long_filter, "seq", split_axis=0, concat_axis=1, tiled=True),
    )
    long_conv = long_convolution(short_whole, filter_whole)
    long_whole = (long_conv + bias_slice[:, None] * short_whole.astype(jnp.float32)).astype(
        jnp.bfloat16
    )
    long_out = lax.all_to_all(long_whole, "seq", split_axis=1, concat_axis=0, tiled=True)
    mixed = (gate_stream.astype(jnp.float32) * long_out.astype(jnp.float32)).astype(jnp.bfloat16)
    mixed_whole = lax.all_gather(mixed, "seq", axis=1, tiled=True)
    owned = lax.all_to_all(upstream, "seq", split_axis=0, concat_axis=1, tiled=True)
    weight_grad = lax.dot_general(
        owned, mixed_whole, (((1,), (1,)), ((), ())), preferred_element_type=jnp.float32
    )
    return (mixed, weight_grad)


def solution(mesh):
    placed = (
        P("chan", "seq"),
        P("chan"),
        P("chan", None),
        P("chan", "seq"),
        P("chan"),
        P("chan", "seq"),
        P(None, "seq"),
    )
    return jax.shard_map(
        shards,
        mesh=mesh,
        in_specs=placed,
        out_specs=(P("chan", "seq"), P("seq", "chan")),
        check_vma=False,
    )
```

profile of v0, /device:TPU:0, one launch (start us, length us, event | category | flops | bytes accessed | tf_op | source)
XLA Modules:
  0.0 184.7 jit_solution(16678184828693716588)
XLA Ops:
  7.2 1.3 fusion.43
  8.4 13.5 %psum.7 = f32[256]{0:T(256)S(1)} all-reduce(f32[256]{0:T(256)S(1)} %fusion.43), channel_id=1, replica_groups=mesh['seq'=8,'chan'=4] {'chan'}, use_global_device_ids=true, to_apply=%region_1.0 | all-reduce | flops 256 | bytes 2048 | tf_op jit(solution)/shard_map/psum | solution.py:120
  21.9 1.2 fusion.45
  23.2 1.3 collective-permute-start
  24.5 4.6 %all-to-all-start.1 = ((bf16[8,128,256]{2,1,0:T(8,128)(2,1)}), bf16[8,128,256]{2,1,0:T(8,128)(2,1)S(1)}, u32[]{:S(2)}, u32[]{:S(2)}) async-start(bf16[8,128,256]{2,1,0:T(8,128)(2,1)} %bitcast.13), calls=%async_computation.1 | async-start | bytes 1048576 | tf_op jit(solution)/shard_map/all_to_all | solution.py:136
  30.0 1.0 copy.57
  32.8 2.2 %copy.56 = bf16[1,1024,383]{1,0,2:T(2,128)(2,1)S(1)} copy(bf16[1,1024,383]{2,1,0:T(8,128)(2,1)S(1)} %maximum_bitcast_fusion) | data formatting | bytes 1568768 | tf_op jit(solution)/shard_map/broadcast_in_dim | solution.py:23
  35.1 12.7 %convolution_convert_fusion = bf16[1,1024,256]{1,0,2:T(2,128)(2,1)S(1)} fusion(bf16[1,1024,383]{1,0,2:T(2,128)(2,1)S(1)} %copy.56, f32[1024,1,128]{0,1,2:T(1,128)} %copy.57), kind=kOutput, calls=%fused_computation.43 | convolution fusion | flops 402915328 | bytes 1832960 | tf_op jit(solution)/shard_map/conv_general_dilated | solution.py:22
  47.8 2.0 %copy.58 = bf16[1,1024,256]{2,1,0:T(8,128)(2,1)} copy(bf16[1,1024,256]{1,0,2:T(2,128)(2,1)S(1)} %convolution_convert_fusion) | data formatting | bytes 1048576 | tf_op jit(solution)/shard_map/convert_element_type | solution.py:133
  49.8 4.2 %all-to-all-start = ((bf16[8,128,256]{2,1,0:T(8,128)(2,1)}), bf16[8,128,256]{2,1,0:T(8,128)(2,1)S(1)}, u32[]{:S(2)}, u32[]{:S(2)}) async-start(bf16[8,128,256]{2,1,0:T(8,128)(2,1)} %bitcast.2), calls=%async_computation | async-start | bytes 1048576 | tf_op jit(solution)/shard_map/all_to_all | solution.py:135
  56.6 1.6 subtract_bitcast_fusion
  58.2 3.3 %fusion.6 = f32[128,64,64]{0,2,1:T(8,128)S(1)} fusion(f32[128,64,64]{0,1,2:T(8,128)S(1)} %get-tuple-element.13), kind=kOutput, calls=%fused_computation.16 | convolution fusion | flops 402710528 | bytes 4194304 | tf_op jit(solution)/shard_map/ckm,jm->ckj/dot_general | solution.py:45
  61.5 3.4 %fusion.31 = f32[128,64,64]{0,2,1:T(8,128)S(1)} fusion(f32[128,64,64]{0,2,1:T(8,128)S(1)} %fusion.6, f32[128,64,64]{0,1,2:T(8,128)S(1)} %get-tuple-element.12), kind=kOutput, calls=%fused_computation.35 | convolution fusion | flops 403234816 | bytes 6291456 | tf_op jit(solution)/shard_map/ckm,jm->ckj/dot_general | solution.py:45
  64.9 3.5 %fusion.8 = f32[128,64,64]{0,2,1:T(8,128)S(1)} fusion(f32[128,64,64]{0,1,2:T(8,128)S(1)} %get-tuple-element.13), kind=kOutput, calls=%fused_computation.18 | convolution fusion | flops 402710528 | bytes 4194304 | tf_op jit(solution)/shard_map/ckm,jm->ckj/dot_general | solution.py:45
  68.5 4.7 %fusion.28 = f32[128,64,64]{0,2,1:T(8,128)} fusion(f32[128,64,64]{0,2,1:T(8,128)S(1)} %fusion.8, f32[128,64,64]{0,1,2:T(8,128)S(1)} %get-tuple-element.12), kind=kOutput, calls=%fused_computation.34 | convolution fusion | flops 403234816 | bytes 6291456 | tf_op jit(solution)/shard_map/ckm,jm->ckj/dot_general | solution.py:45
  75.2 1.6 fusion
  76.8 3.3 %fusion.16 = f32[128,64,64]{0,2,1:T(8,128)S(1)} fusion(f32[128,64,64]{0,1,2:T(8,128)S(1)} %get-tuple-element.15), kind=kOutput, calls=%fused_computation.26 | convolution fusion | flops 402710528 | bytes 4194304 | tf_op jit(solution)/shard_map/ckm,jm->ckj/dot_general | solution.py:45
  80.1 3.5 %fusion.14 = f32[128,64,64]{0,2,1:T(8,128)S(1)} fusion(f32[128,64,64]{0,1,2:T(8,128)S(1)} %get-tuple-element.15), kind=kOutput, calls=%fused_computation.24 | convolution fusion | flops 402710528 | bytes 4194304 | tf_op jit(solution)/shard_map/ckm,jm->ckj/dot_general | solution.py:45
  83.6 3.3 %fusion.22 = f32[128,64,64]{0,2,1:T(8,128)S(1)} fusion(f32[128,64,64]{0,2,1:T(8,128)S(1)} %fusion.16, f32[128,64,64]{0,1,2:T(8,128)S(1)} %get-tuple-element.14), kind=kOutput, calls=%fused_computation.32 | convolution fusion | flops 403234816 | bytes 6291456 | tf_op jit(solution)/shard_map/ckm,jm->ckj/dot_general | solution.py:45
  87.0 4.0 %multiply_add_fusion.1 = (f32[128,64,64]{0,2,1:T(8,128)S(1)}, f32[128,64,64]{0,2,1:T(8,128)S(1)}) fusion(f32[128,64,64]{0,2,1:T(8,128)S(1)} %copy-done, f32[128,64,64]{0,2,1:T(8,128)S(1)} %fusion.22, f32[128,64,64]{0,2,1:T(8,128)S(1)} %fusion.31, f32[128,64,64]{0,2,1:T(8,128)S(1)} %fusion.14, f32[128,64,64]{0,1,2:T(8,128)S(1)} %get-tuple-element.14), kind=kOutput, calls=%fused_computation.12 | convolution fusion | flops 406380544 | bytes 14680064 | tf_op jit(solution)/shard_map/ckm,jm->ckj/dot_general | solution.py:45
  91.0 2.2 %fusion.65 = f32[128,64,64]{0,2,1:T(8,128)S(1)} fusion(f32[128,64,64]{0,2,1:T(8,128)S(1)} %get-tuple-element.9), kind=kOutput, calls=%fused_computation.79 | convolution fusion | flops 402710528 | bytes 4194304 | tf_op jit(solution)/shard_map/ckj,mj->ckm/dot_general | solution.py:45
  93.1 2.5 %fusion.61 = f32[128,64,64]{0,2,1:T(8,128)S(1)} fusion(f32[128,64,64]{0,2,1:T(8,128)S(1)} %get-tuple-element.9), kind=kOutput, calls=%fused_computation.75 | convolution fusion | flops 402710528 | bytes 4194304 | tf_op jit(solution)/shard_map/ckj,mj->ckm/dot_general | solution.py:45
  95.7 2.2 %convolution_subtract_fusion = f32[128,64,64]{0,2,1:T(8,128)S(1)} fusion(f32[128,64,64]{0,2,1:T(8,128)S(1)} %fusion.65, f32[128,64,64]{0,2,1:T(8,128)S(1)} %get-tuple-element.8), kind=kOutput, calls=%fused_computation.38 | convolution fusion | flops 403234816 | bytes 6291456 | tf_op jit(solution)/shard_map/ckj,mj->ckm/dot_general | solution.py:45
  97.8 3.2 %multiply_subtract_fusion = (f32[128,64,64]{0,2,1:T(8,128)S(1)}, f32[128,64,64]{0,2,1:T(8,128)S(1)}) fusion(f32[128,64,64]{0,2,1:T(8,128)S(1)} %convolution_subtract_fusion, f32[64,64]{1,0:T(8,128)S(1)} %get-tuple-element.16, f32[64,64]{1,0:T(8,128)S(1)} %get-tuple-element.17, f32[128,64,64]{0,2,1:T(8,128)S(1)} %fusion.61, ...), kind=kOutput, calls=%fused_computation.11 | convolution fusion | flops 406380544 | bytes 10518528 | tf_op jit(solution)/shard_map/ckj,mj->ckm/dot_general | solution.py:45
  101.0 2.5 %fusion.2 = f32[128,64,32]{0,2,1:T(8,128)S(1)} fusion(f32[128,64,64]{0,2,1:T(8,128)S(1)} %get-tuple-element.11), kind=kOutput, calls=%fused_computation.6 | convolution fusion | flops 201355264 | bytes 3145728 | tf_op jit(solution)/shard_map/nk,ckm->cnm/dot_general | solution.py:45
  103.5 2.5 %fusion.40 = f32[128,32,64]{0,1,2:T(8,128)S(1)} fusion(f32[128,64,32]{0,2,1:T(8,128)S(1)} %fusion.2, f32[128,64,64]{0,2,1:T(8,128)S(1)} %get-tuple-element.10), kind=kOutput, calls=%fused_computation.46 | convolution fusion | flops 201879552 | bytes 4194304 | tf_op jit(solution)/shard_map/nk,ckm->cnm/dot_general | solution.py:45
  107.4 13.7 %all_to_all.58 = bf16[128,8,256]{2,0,1:T(8,128)(2,1)S(1)} all-to-all(bf16[128,8,256]{2,0,1:T(8,128)(2,1)S(1)} %add_convert_fusion), channel_id=1, replica_groups=mesh['seq'=8,'chan'=4] {'seq'}, dimensions={1} | all-to-all | bytes 1048576 | tf_op jit(solution)/shard_map/all_to_all | solution.py:142
  122.0 38.7 %all_to_all.59 = bf16[8,512,256]{2,1,0:T(8,128)(2,1)S(1)} all-to-all(bf16[8,512,256]{2,1,0:T(8,128)(2,1)} %bitcast.121), channel_id=1, replica_groups=mesh['seq'=8,'chan'=4] {'seq'}, dimensions={0} | all-to-all | bytes 4194304 | tf_op jit(solution)/shard_map/all_to_all | solution.py:145
  160.7 2.4 %copy.85 = bf16[512,8,256]{0,2,1:T(8,128)(2,1)} copy(bf16[512,8,256]{2,0,1:T(8,128)(2,1)S(1)} %bitcast.118) | data formatting | bytes 4194304 | tf_op jit(solution)/shard_map/all_to_all | solution.py:145
  163.1 7.5 %all-gather.2.cloned.1.call-done = bf16[1024,2048]{1,0:T(8,128)(2,1)} async-done(((bf16[1024,256]{1,0:T(8,128)(2,1)}), bf16[1024,2048]{1,0:T(8,128)(2,1)}) %all-gather.2.cloned.1.call-update) | async-done | bytes 4194320 | tf_op jit(solution)/shard_map/all_gather | solution.py:144
  170.6 5.2 %convolution_bitcast_fusion = f32[512,1024]{0,1:T(8,128)S(1)} fusion(bf16[1024,2048]{1,0:T(8,128)(2,1)} %all-gather.2.cloned.1.call-done, bf16[512,2048]{0,1:T(8,128)(2,1)} %bitcast.122), kind=kOutput, calls=%fused_computation.36 | convolution fusion | flops 2147483648 | bytes 8388608 | tf_op jit(solution)/shard_map/dot_general | solution.py:146
  175.8 1.8 copy.86
  (34 shorter events, 9.4 us)
Async XLA Ops:
  7.2 22.1 %copy-start.2 = (f32[1024,128]{1,0:T(8,128)S(1)}, f32[1024,128]{1,0:T(8,128)}, u32[]{:S(2)}) copy-start(f32[1024,128]{1,0:T(8,128)} %param.9) | copy-start | bytes 1572868
  23.2 9.1 %collective-permute-start = (bf16[1024,128]{1,0:T(8,128)(2,1)S(1)}, bf16[1024,128]{1,0:T(8,128)(2,1)S(1)}, u32[]{:S(2)}, u32[]{:S(2)}) collective-permute-start(bf16[1024,128]{1,0:T(8,128)(2,1)S(1)} %slice.8), channel_id=1, source_target_pairs={{0,4},{4,8},{8,12},{12,16},{16,20},{20,24},{24,28},{1,5},{5,9},{9,... | collective-permute-start | bytes 786440 | tf_op jit(solution)/shard_map/ppermute | solution.py:17
  24.5 25.3 %all-to-all-start.1 = ((bf16[8,128,256]{2,1,0:T(8,128)(2,1)}), bf16[8,128,256]{2,1,0:T(8,128)(2,1)S(1)}, u32[]{:S(2)}, u32[]{:S(2)}) async-start(bf16[8,128,256]{2,1,0:T(8,128)(2,1)} %bitcast.13), calls=%async_computation.1 | async-start | bytes 1048576 | tf_op jit(solution)/shard_map/all_to_all | solution.py:136
  49.8 23.4 %all-to-all-start = ((bf16[8,128,256]{2,1,0:T(8,128)(2,1)}), bf16[8,128,256]{2,1,0:T(8,128)(2,1)S(1)}, u32[]{:S(2)}, u32[]{:S(2)}) async-start(bf16[8,128,256]{2,1,0:T(8,128)(2,1)} %bitcast.2), calls=%async_computation | async-start | bytes 1048576 | tf_op jit(solution)/shard_map/all_to_all | solution.py:135
  54.0 116.6 %all-gather.2.cloned.1.call-start = ((), (), s32[]{:S(2)}) async-start(), calls=%async_computation.4 | async-start | bytes 4718592 | tf_op jit(solution)/shard_map/all_gather | solution.py:144
  83.6 3.3 %copy-start = (f32[128,64,64]{0,2,1:T(8,128)S(1)}, f32[128,64,64]{0,2,1:T(8,128)}, u32[]{:S(2)}) copy-start(f32[128,64,64]{0,2,1:T(8,128)} %fusion.28) | copy-start | bytes 6291460
  107.2 13.9 %copy-start.1 = (bf16[1024,256]{1,0:T(8,128)(2,1)S(1)}, bf16[1024,256]{1,0:T(8,128)(2,1)}, u32[]{:S(2)}) copy-start(bf16[1024,256]{1,0:T(8,128)(2,1)} %param.12) | copy-start | bytes 1572868
Sparse Core Ops, SparseCore 0:
  122.1 48.4 all-gather.1
where the time goes:
time: 188 us; the launch traced here: 185 us
  matrix products  68.7 us (37%)
  blocking collectives  65.9 us (35%)
  between operations  14.5 us (8%)
  local copies, waits for them, and re-layouts  12.9 us (7%)
  starting transfers between devices  10.7 us (6%)
  waiting for transfers between devices  7.52 us (4%)
  other arithmetic  4.45 us (2%)
    dot_general x14, matrix products, product_einsum(): return jnp.einsum(form, left, right, precision=lax.Precision.HIGHEST)  44.1 us
    all_to_all x1, blocking collectives, shards(): lax.all_to_all(upstream, 'seq', split_axis=0, concat_axis=1, tiled=True)  38.7 us
    all_to_all x1, blocking collectives, shards(): lax.all_to_all(long_whole, 'seq', split_axis=1, concat_axis=0, tiled=True)  13.7 us
    psum x1, blocking collectives, shards(): squares = lax.psum(partial_squares, 'chan')  13.5 us
    conv_general_dilated x1, matrix products, short_conv(): lax.conv_general_dilated(padded[None], kernel, (1,), 'VALID', dimension_n...  12.7 us
    all_gather x1, waiting for transfers between devices, shards(): mixed_whole = lax.all_gather(mixed, 'seq', axis=1, tiled=True)  7.5 us
    dot_general x1, matrix products, shards(): lax.dot_general(owned, mixed_whole, (((1,), (1,)), ((), ())), preferred_e...  5.18 us
    all_to_all x1, starting transfers between devices, shards(): lax.all_to_all(long_filter, 'seq', split_axis=0, concat_axis=1, tiled=True)  4.62 us
  transfers between devices with their start and end apart: 4, of which 1 were waited for; matrix products, arithmetic and copies ran while one was open for 22% of the time, Pallas kernels for 0%

commit v1 on v0

v1 whole, which is shorter than its diff:
```python
import functools

import jax
import jax.numpy as jnp
from jax import lax
from jax.experimental import pallas as pl
from jax.experimental.pallas import tpu as pltpu
from jax.sharding import PartitionSpec as P

EPSILON = 1e-05
BF16 = jnp.bfloat16
F32 = jnp.float32


def body(
    n,
    nz,
    groups,
    hidden,
    gain,
    taps,
    filt,
    bias,
    gate,
    upstream,
    out_mixed,
    out_grad,
    hidden_own,
    land_hidden,
    land_filt,
    land_gate,
    taps_own,
    sq_land,
    inv_land,
    owned,
    whole,
    xs,
    hs,
    gs,
    ms,
    local_sem,
    hid_send,
    hid_recv,
    fil_send,
    fil_recv,
    gat_send,
    gat_recv,
    up_send,
    up_recv,
    sq_send,
    sq_recv,
    inv_send,
    inv_recv,
    mix_send,
    mix_recv,
    fwd_send,
):
    me = lax.axis_index("seq")
    mz = lax.axis_index("chan")
    wide, cols = hidden.shape
    width = wide // n
    rows = upstream.shape[0] // n
    block = taps.shape[1]
    per = cols // block
    blocks = n * per
    total = wide * nz
    share = width // groups
    seq_len = n * cols

    def remote(src, dst, send, recv, peer, axis="seq"):
        return pltpu.make_async_remote_copy(
            src_ref=src,
            dst_ref=dst,
            send_sem=send,
            recv_sem=recv,
            device_id={axis: peer},
            device_id_type=pl.DeviceIdType.MESH,
        )

    local = [
        pltpu.make_async_copy(hidden, hidden_own, local_sem.at[0]),
        pltpu.make_async_copy(
            hidden.at[pl.ds(me * width, width)], land_hidden.at[me], local_sem.at[1]
        ),
        pltpu.make_async_copy(taps.at[pl.ds(me * width, width)], taps_own, local_sem.at[2]),
        pltpu.make_async_copy(filt.at[pl.ds(me * width, width)], land_filt.at[me], local_sem.at[3]),
        pltpu.make_async_copy(gate.at[pl.ds(me * width, width)], land_gate.at[me], local_sem.at[4]),
        pltpu.make_async_copy(
            upstream.at[pl.ds(me * rows, rows)],
            owned.at[:, pl.ds(pl.multiple_of(me * cols, 128), cols)],
            local_sem.at[5],
        ),
    ]
    for copy in local:
        copy.start()

    barrier = pltpu.get_barrier_semaphore()
    for r in range(1, n):
        pl.semaphore_signal(
            barrier,
            inc=1,
            device_id={"seq": (me + r) % n},
            device_id_type=pl.DeviceIdType.MESH,
        )
    for r in range(1, nz):
        pl.semaphore_signal(
            barrier,
            inc=1,
            device_id={"chan": (mz + r) % nz},
            device_id_type=pl.DeviceIdType.MESH,
        )
    pl.semaphore_wait(barrier, n + nz - 2)

    sends = []

    def spread(source, land, send, recv):
        for r in range(1, n):
            peer = (me + r) % n
            copy = remote(
                source.at[pl.ds(peer * width, width)], land.at[me], send.at[r], recv.at[me], peer
            )
            copy.start()
            sends.append(copy)

    spread(hidden, land_hidden, hid_send, hid_recv)
    spread(filt, land_filt, fil_send, fil_recv)
    spread(gate, land_gate, gat_send, gat_recv)
    my_cols = pl.ds(pl.multiple_of(me * cols, 128), cols)
    for r in range(1, n):
        peer = (me + r) % n
        copy = remote(
            upstream.at[pl.ds(peer * rows, rows)],
            owned.at[:, my_cols],
            up_send.at[r],
            up_recv.at[me],
            peer,
        )
        copy.start()
        sends.append(copy)

    local[0].wait()

    def add_square(i, acc):
        part = hidden_own[pl.ds(pl.multiple_of(i * 32, 32), 32), :].astype(F32)
        part = part * part
        return acc + (part[0:8] + part[8:16]) + (part[16:24] + part[24:32])

    sq_land[mz] = lax.fori_loop(0, wide // 32, add_square, jnp.zeros((8, cols), F32), unroll=4)
    for r in range(1, nz):
        peer = (mz + r) % nz
        copy = remote(
            sq_land.at[mz], sq_land.at[mz], sq_send.at[r], sq_recv.at[mz], peer, "chan"
        )
        copy.start()
        sends.append(copy)
    for r in range(1, nz):
        peer = (mz + r) % nz
        remote(
            sq_land.at[mz], sq_land.at[peer], sq_send.at[r], sq_recv.at[peer], peer, "chan"
        ).wait_recv()
    squares = sq_land[0]
    for z in range(1, nz):
        squares = squares + sq_land[z]
    squares = jnp.sum(squares, axis=0, keepdims=True)
    inverse = lax.rsqrt(squares / total + EPSILON)
    inv_land[me] = jnp.broadcast_to(inverse, (8, cols))
    for r in range(1, n):
        peer = (me + r) % n
        copy = remote(inv_land.at[me], inv_land.at[me], inv_send.at[r], inv_recv.at[me], peer)
        copy.start()
        sends.append(copy)

    def arrived(land, send, recv):
        for r in range(1, n):
            peer = (me + r) % n
            remote(land.at[me], land.at[peer], send.at[r], recv.at[peer], peer).wait_recv()

    local[1].wait()
    local[2].wait()
    local[3].wait()
    local[4].wait()
    arrived(land_hidden, hid_send, hid_recv)
    arrived(inv_land, inv_send, inv_recv)
    for p in range(n):
        for k in range(per):
            lanes = slice(k * block, (k + 1) * block)
            spot = slice((p * per + k) * width, (p * per + k + 1) * width)
            xs[spot, :] = land_hidden[p, :, lanes].astype(F32) * inv_land[p, 0:1, lanes]
    arrived(land_filt, fil_send, fil_recv)
    for p in range(n):
        for k in range(per):
            lanes = slice(k * block, (k + 1) * block)
            spot = slice((p * per + k) * width, (p * per + k + 1) * width)
            hs[spot, :] = land_filt[p, :, lanes].astype(F32)
    arrived(land_gate, gat_send, gat_recv)
    for p in range(n):
        for k in range(per):
            lanes = slice(k * block, (k + 1) * block)
            spot = slice((p * per + k) * width, (p * per + k + 1) * width)
            gs[spot, :] = land_gate[p, :, lanes].astype(F32)

    lane_at = lax.broadcasted_iota(jnp.int32, (block, block), 1)
    row_at = lax.broadcasted_iota(jnp.int32, (block, block), 0)
    causal = lane_at >= row_at
    block_at = lax.broadcasted_iota(jnp.int32, (blocks, block), 0)

    def circulant(row):
        return pltpu.roll(
            jnp.broadcast_to(row, (block, block)), 0, 1, stride=1, stride_axis=0
        )

    def later(value, by):
        if by == 0:
            return value
        return jnp.where(block_at >= by, pltpu.roll(value, by, 0), 0.0)

    def channel(c, carry):
        mine = pl.ds(c, blocks, stride=width)
        x = (xs[mine, :] * gain[me * width + c]).astype(BF16)
        turned = circulant(taps_own[pl.ds(c, 1), :])
        now = jnp.where(causal, turned, 0.0).astype(BF16)
        before = jnp.where(causal, 0.0, turned).astype(BF16)
        pair = jnp.concatenate([x, later(x.astype(F32), 1).astype(BF16)], axis=1)
        short = jnp.dot(
            pair, jnp.concatenate([now, before], axis=0), preferred_element_type=F32
        )
        short = short.astype(BF16).astype(F32)
        acc = bias[me * width + c] * short
        held = jnp.zeros((block, block), F32)
        step = 2 if blocks % 2 == 0 else 1
        for d in range(0, blocks, step):
            signal, table = [], []
            for e in range(d, d + step):
                turned = circulant(hs[pl.ds(e * width + c, 1), :])
                table.append(jnp.where(causal, turned, held).astype(BF16))
                held = turned
                signal.append(later(short, e).astype(BF16))
            acc = acc + jnp.dot(
                jnp.concatenate(signal, axis=1),
                jnp.concatenate(table, axis=0),
                preferred_element_type=F32,
            )
        ms[mine, :] = gs[mine, :] * acc.astype(BF16).astype(F32)
        return carry

    other = me + 1 - 2 * (me % 2)

    def piece(src, g):
        return whole.at[src, pl.ds(g * share, share)]

    def forward(g):
        for k in range(1, n // 2):
            source = (me + 2 * k) % n
            remote(
                piece(me, g), piece(source, g), mix_send.at[g, k], mix_recv.at[g, source], source
            ).wait_recv()
            copy = remote(
                piece(source, g),
                piece(source, g),
                fwd_send.at[g, k],
                mix_recv.at[g, source],
                other,
            )
            copy.start()
            sends.append(copy)

    for g in range(groups):
        lax.fori_loop(g * share, (g + 1) * share, channel, 0)
        for b in range(blocks):
            start = b * width + g * share
            whole[me, g * share : (g + 1) * share, b * block : (b + 1) * block] = ms[
                start : start + share, :
            ].astype(BF16)
        for k in range(1, n // 2):
            peer = (me + 2 * k) % n
            copy = remote(
                piece(me, g), piece(me, g), mix_send.at[g, k], mix_recv.at[g, me], peer
            )
            copy.start()
            sends.append(copy)
        copy = remote(piece(me, g), piece(me, g), mix_send.at[g, 0], mix_recv.at[g, me], other)
        copy.start()
        sends.append(copy)
        if g > 0:
            forward(g - 1)
    forward(groups - 1)

    local[5].wait()
    for r in range(1, n):
        peer = (me + r) % n
        remote(
            upstream.at[pl.ds(0, rows)],
            owned.at[:, pl.ds(pl.multiple_of(peer * cols, 128), cols)],
            up_send.at[r],
            up_recv.at[peer],
            peer,
        ).wait_recv()

    for k in range(n // 2):
        source = (other + 2 * k) % n
        for g in range(groups):
            remote(
                piece(me, g), piece(source, g), mix_send.at[g, 0], mix_recv.at[g, source], other
            ).wait_recv()

    for p in range(n):
        out_mixed[p * width : (p + 1) * width, :] = whole[p, :, my_cols]

    sources = max(2, 128 // width)
    tile = min(rows, 128)
    for q in range(n // sources):
        right = whole[q * sources : (q + 1) * sources].reshape(sources * width, seq_len)

        def multiply(i, carry):
            at = pl.ds(pl.multiple_of(i * tile, tile), tile)
            out_grad[at, q * sources * width : (q + 1) * sources * width] = lax.dot_general(
                owned[at, :], right, (((1,), (1,)), ((), ())), preferred_element_type=F32
            )
            return carry

        lax.fori_loop(0, rows // tile, multiply, 0)

    for copy in sends:
        copy.wait_send()


def shards(hidden_states, norm_gain, short_filter, long_filter, long_bias, gate_stream, upstream):
    n = lax.axis_size("seq")
    nz = lax.axis_size("chan")
    wide, cols = hidden_states.shape
    width = wide // n
    rows = upstream.shape[0] // n
    seq_len = cols * n
    groups = max(1, width // 32)
    block = short_filter.shape[1]
    anywhere = pl.BlockSpec(memory_space=pl.ANY)
    scalars = pl.BlockSpec(memory_space=pltpu.SMEM)
    vmem = pl.BlockSpec(memory_space=pltpu.VMEM)
    dma = pltpu.SemaphoreType.DMA
    flat = (seq_len // block * width, block)
    return pl.pallas_call(
        functools.partial(body, n, nz, groups),
        out_shape=(
            jax.ShapeDtypeStruct((wide, cols), BF16),
            jax.ShapeDtypeStruct((rows, wide), F32),
        ),
        in_specs=[anywhere, scalars, anywhere, anywhere, scalars, anywhere, anywhere],
        out_specs=(vmem, vmem),
        scratch_shapes=[
            pltpu.VMEM((wide, cols), BF16),
            pltpu.VMEM((n, width, cols), BF16),
            pltpu.VMEM((n, width, cols), BF16),
            pltpu.VMEM((n, width, cols), BF16),
            pltpu.VMEM((width, block), F32),
            pltpu.VMEM((nz, 8, cols), F32),
            pltpu.VMEM((n, 8, cols), F32),
            pltpu.VMEM((rows, seq_len), BF16),
            pltpu.VMEM((n, width, seq_len), BF16),
            pltpu.VMEM(flat, F32),
            pltpu.VMEM(flat, F32),
            pltpu.VMEM(flat, F32),
            pltpu.VMEM(flat, F32),
            dma((6,)),
            dma((n,)),
            dma((n,)),
            dma((n,)),
            dma((n,)),
            dma((n,)),
            dma((n,)),
            dma((n,)),
            dma((n,)),
            dma((nz,)),
            dma((nz,)),
            dma((n,)),
            dma((n,)),
            dma((groups, n)),
            dma((groups, n)),
            dma((groups, n)),
        ],
        compiler_params=pltpu.CompilerParams(
            collective_id=0, has_side_effects=True, vmem_limit_bytes=48 * 1024 * 1024
        ),
        name="hyena",
    )(hidden_states, norm_gain, short_filter, long_filter, long_bias, gate_stream, upstream)


def solution(mesh):
    placed = (
        P("chan", "seq"),
        P("chan"),
        P("chan", None),
        P("chan", "seq"),
        P("chan"),
        P("chan", "seq"),
        P(None, "seq"),
    )
    return jax.shard_map(
        shards,
        mesh=mesh,
        in_specs=placed,
        out_specs=(P("chan", "seq"), P("seq", "chan")),
        check_vma=False,
    )
```

time: 188 us -> 127 us (0.68); the launches traced: 185 us -> 126 us
  Pallas kernels: 0 us -> 118 us
  matrix products: 68.7 us -> 0 us
  blocking collectives: 65.9 us -> 0 us
  between operations: 14.5 us -> 0.65 us
  starting transfers between devices: 10.7 us -> 0 us
  waiting for transfers between devices: 7.52 us -> 0 us
  local copies, waits for them, and re-layouts: 12.9 us -> 7.64 us
  other arithmetic: 4.45 us -> 0 us
    pallas_call x0 -> x1, Pallas kernels: none -> 118 us  [shards(): pl.pallas_call(functools.partial(body, n, nz, groups), out_shape=(jax.Sha...]
    dot_general x23 -> x0, matrix products: 55.9 us -> none  [the longest x14 44.1 us: product_einsum(): return jnp.einsum(form, left, right, precision=lax.Precision.HIGHEST)]
    all_to_all x2 -> x0, blocking collectives: 52.4 us -> none  [the longest x1 38.7 us: shards(): lax.all_to_all(upstream, 'seq', split_axis=0, concat_axis=1, tiled=True)]
    psum x1 -> x0, blocking collectives: 13.5 us -> none  [shards(): squares = lax.psum(partial_squares, 'chan')]
    conv_general_dilated x1 -> x0, matrix products: 12.7 us -> none  [short_conv(): lax.conv_general_dilated(padded[None], kernel, (1,), 'VALID', dimension_n...]
    all_to_all x2 -> x0, starting transfers between devices: 8.82 us -> none  [the longest x1 4.62 us: shards(): lax.all_to_all(long_filter, 'seq', split_axis=0, concat_axis=1, tiled=True)]
    all_gather x1 -> x0, waiting for transfers between devices: 7.5 us -> none  [shards(): mixed_whole = lax.all_gather(mixed, 'seq', axis=1, tiled=True)]
    unnamed x7 -> x14, local copies, waits for them, and re-layouts: 1.83 us -> 7.64 us
  transfers between devices with their start and end apart: 4 -> 0, of which waited for: 1 -> 0; matrix products, arithmetic and copies ran while one was open for 22% -> 0% of each run, Pallas kernels for 0% -> 0%
where the time goes in v1:
time: 127 us; the launch traced here: 126 us
  Pallas kernels  118 us (93%)
  local copies, waits for them, and re-layouts  7.64 us (6%)
    pallas_call x1, Pallas kernels, shards(): pl.pallas_call(functools.partial(body, n, nz, groups), out_shape=(jax.Sha...  118 us
    unnamed x14, local copies, waits for them, and re-layouts  7.64 us

profile of v1, /device:TPU:0, one launch (start us, length us, event | category | flops | bytes accessed | tf_op | source)
XLA Modules:
  0.0 125.9 jit_solution(10294419698527102330)
XLA Ops:
  0.6 0.0 copy-start
  0.6 1.0 copy-done
  1.7 0.0 copy-start.1
  1.7 1.0 copy-done.1
  2.7 0.0 copy-start.2
  2.7 1.0 copy-done.2
  3.8 0.0 copy-start.3
  3.8 1.0 copy-done.3
  4.8 0.0 copy-start.4
  4.8 0.7 copy-done.4
  5.5 0.0 copy-start.5
  5.5 0.7 copy-done.5
  6.2 117.6 %hyena.1 = (bf16[1024,256]{1,0:T(8,128)(2,1)S(1)}, f32[512,1024]{1,0:T(8,128)S(1)}) custom-call(bf16[1024,256]{1,0:T(8,128)(2,1)S(1)} %copy-done, f32[1024]{0:T(1024)S(1)} %copy-done.4, f32[1024,128]{1,0:T(8,128)S(1)} %copy-done.1, bf16[1024,256]{1,0:T(8,128)(2,1)S(1)} %copy-done.2, f32[1024]{0:T(1024)S(1)} %copy-done.5, bf16[1024,256]{1,0:T(8,128)(2,1)S(1)} %copy-done.3, ...), custom_call_target="tpu_custom_call" | custom-call | tf_op jit(solution)/shard_map/hyena/pallas_call | solution.py:341
  123.8 0.8 copy.11
  124.6 1.3 %copy.12 = f32[512,1024]{1,0:T(8,128)} copy(f32[512,1024]{1,0:T(8,128)S(1)} %get-tuple-element.5) | data formatting | bytes 4194304
Async XLA Ops:
  0.6 1.0 copy-start
  1.7 1.0 copy-start.1
  2.7 1.0 copy-start.2
  3.8 1.0 copy-start.3
  4.8 0.7 copy-start.4
  5.5 0.7 copy-start.5

commit v2 on v1

--- a/solution.py
+++ b/solution.py
@@ -47,6 +47,10 @@
     gat_recv,
     up_send,
     up_recv,
+    part_send,
+    part_recv,
+    plane_send,
+    plane_recv,
     sq_send,
     sq_recv,
     inv_send,
@@ -65,6 +69,10 @@
     blocks = n * per
     total = wide * nz
     share = width // groups
+    part = rows * 3 // 4 // nz // 16 * 16
+    half = rows - part * nz
+    part_rows = pl.ds(pl.multiple_of(half + mz * part, 16), part)
+    my_cols = pl.ds(pl.multiple_of(me * cols, 128), cols)
     seq_len = n * cols
 
     def remote(src, dst, send, recv, peer, axis="seq"):
@@ -86,9 +94,12 @@
         pltpu.make_async_copy(filt.at[pl.ds(me * width, width)], land_filt.at[me], local_sem.at[3]),
         pltpu.make_async_copy(gate.at[pl.ds(me * width, width)], land_gate.at[me], local_sem.at[4]),
         pltpu.make_async_copy(
-            upstream.at[pl.ds(me * rows, rows)],
-            owned.at[:, pl.ds(pl.multiple_of(me * cols, 128), cols)],
-            local_sem.at[5],
+            upstream.at[pl.ds(me * rows, half)], owned.at[0:half, my_cols], local_sem.at[5]
+        ),
+        pltpu.make_async_copy(
+            upstream.at[pl.ds(me * rows + half + mz * part, part)],
+            owned.at[part_rows, my_cols],
+            local_sem.at[6],
         ),
     ]
     for copy in local:
@@ -123,21 +134,6 @@
             sends.append(copy)
 
     spread(hidden, land_hidden, hid_send, hid_recv)
-    spread(filt, land_filt, fil_send, fil_recv)
-    spread(gate, land_gate, gat_send, gat_recv)
-    my_cols = pl.ds(pl.multiple_of(me * cols, 128), cols)
-    for r in range(1, n):
-        peer = (me + r) % n
-        copy = remote(
-            upstream.at[pl.ds(peer * rows, rows)],
-            owned.at[:, my_cols],
-            up_send.at[r],
-            up_recv.at[me],
-            peer,
-        )
-        copy.start()
-        sends.append(copy)
-
     local[0].wait()
 
     def add_square(i, acc):
@@ -167,6 +163,31 @@
     for r in range(1, n):
         peer = (me + r) % n
         copy = remote(inv_land.at[me], inv_land.at[me], inv_send.at[r], inv_recv.at[me], peer)
+        copy.start()
+        sends.append(copy)
+
+    spread(filt, land_filt, fil_send, fil_recv)
+    spread(gate, land_gate, gat_send, gat_recv)
+    for r in range(1, n):
+        peer = (me + r) % n
+        copy = remote(
+            upstream.at[pl.ds(peer * rows + half + mz * part, part)],
+            owned.at[part_rows, my_cols],
+            part_send.at[r],
+            part_recv.at[me],
+            peer,
+        )
+        copy.start()
+        sends.append(copy)
+    for r in range(1, n):
+        peer = (me + r) % n
+        copy = remote(
+            upstream.at[pl.ds(peer * rows, half)],
+            owned.at[0:half, my_cols],
+            up_send.at[r],
+            up_recv.at[me],
+            peer,
+        )
         copy.start()
         sends.append(copy)
 
@@ -264,8 +285,32 @@
             copy.start()
             sends.append(copy)
 
+    def share_part():
+        local[6].wait()
+        for r in range(1, n):
+            peer = (me + r) % n
+            remote(
+                upstream.at[pl.ds(0, part)],
+                owned.at[part_rows, pl.ds(pl.multiple_of(peer * cols, 128), cols)],
+                part_send.at[r],
+                part_recv.at[peer],
+                peer,
+            ).wait_recv()
+        for r in range(1, nz):
+            peer = (mz + r) % nz
+            copy = remote(
+                owned.at[part_rows],
+                owned.at[part_rows],
+                plane_send.at[r],
+                plane_recv.at[mz],
+                peer,
+                "chan",
+            )
+            copy.start()
+            sends.append(copy)
+
     for g in range(groups):
-        lax.fori_loop(g * share, (g + 1) * share, channel, 0)
+        lax.fori_loop(g * share, (g + 1) * share, channel, 0, unroll=8)
         for b in range(blocks):
             start = b * width + g * share
             whole[me, g * share : (g + 1) * share, b * block : (b + 1) * block] = ms[
@@ -281,6 +326,8 @@
         copy = remote(piece(me, g), piece(me, g), mix_send.at[g, 0], mix_recv.at[g, me], other)
         copy.start()
         sends.append(copy)
+        if g == 0:
+            share_part()
         if g > 0:
             forward(g - 1)
     forward(groups - 1)
@@ -289,11 +336,22 @@
     for r in range(1, n):
         peer = (me + r) % n
         remote(
-            upstream.at[pl.ds(0, rows)],
-            owned.at[:, pl.ds(pl.multiple_of(peer * cols, 128), cols)],
+            upstream.at[pl.ds(0, half)],
+            owned.at[0:half, pl.ds(pl.multiple_of(peer * cols, 128), cols)],
             up_send.at[r],
             up_recv.at[peer],
             peer,
+        ).wait_recv()
+
+    for r in range(1, nz):
+        peer = (mz + r) % nz
+        remote(
+            owned.at[part_rows],
+            owned.at[pl.ds(pl.multiple_of(half + peer * part, 16), part)],
+            plane_send.at[r],
+            plane_recv.at[peer],
+            peer,
+            "chan",
         ).wait_recv()
 
     for k in range(n // 2):
@@ -360,15 +418,19 @@
             pltpu.VMEM(flat, F32),
             pltpu.VMEM(flat, F32),
             pltpu.VMEM(flat, F32),
-            dma((6,)),
-            dma((n,)),
-            dma((n,)),
-            dma((n,)),
-            dma((n,)),
-            dma((n,)),
-            dma((n,)),
-            dma((n,)),
-            dma((n,)),
+            dma((7,)),
+            dma((n,)),
+            dma((n,)),
+            dma((n,)),
+            dma((n,)),
+            dma((n,)),
+            dma((n,)),
+            dma((n,)),
+            dma((n,)),
+            dma((n,)),
+            dma((n,)),
+            dma((nz,)),
+            dma((nz,)),
             dma((nz,)),
             dma((nz,)),
             dma((n,)),

time: 127 us -> 86 us (0.68)
  Pallas kernels: 118 us -> 77.3 us
    pallas_call x1, Pallas kernels: 118 us -> 77.3 us  [shards(): pl.pallas_call(functools.partial(body, n, nz, groups), out_shape=(jax.Sha...]
where the time goes in v2:
time: 86 us; the launch traced here: 85.6 us
  Pallas kernels  77.3 us (90%)
  local copies, waits for them, and re-layouts  7.64 us (9%)
    pallas_call x1, Pallas kernels, shards(): pl.pallas_call(functools.partial(body, n, nz, groups), out_shape=(jax.Sha...  77.3 us
    unnamed x14, local copies, waits for them, and re-layouts  7.64 us

profile of v2, /device:TPU:0, one launch (start us, length us, event | category | flops | bytes accessed | tf_op | source)
XLA Modules:
  0.0 85.6 jit_solution(13636163031598039605)
XLA Ops:
  0.6 0.0 copy-start
  0.6 1.0 %copy-done = bf16[1024,256]{1,0:T(8,128)(2,1)S(1)} copy-done((bf16[1024,256]{1,0:T(8,128)(2,1)S(1)}, bf16[1024,256]{1,0:T(8,128)(2,1)}, u32[]{:S(2)}) %copy-start) | copy-done | bytes 524312
  1.7 0.0 copy-start.1
  1.7 1.0 %copy-done.1 = f32[1024,128]{1,0:T(8,128)S(1)} copy-done((f32[1024,128]{1,0:T(8,128)S(1)}, f32[1024,128]{1,0:T(8,128)}, u32[]{:S(2)}) %copy-start.1) | copy-done | bytes 524312
  2.7 0.0 copy-start.2
  2.7 1.0 %copy-done.2 = bf16[1024,256]{1,0:T(8,128)(2,1)S(1)} copy-done((bf16[1024,256]{1,0:T(8,128)(2,1)S(1)}, bf16[1024,256]{1,0:T(8,128)(2,1)}, u32[]{:S(2)}) %copy-start.2) | copy-done | bytes 524312
  3.8 0.0 copy-start.3
  3.8 1.0 %copy-done.3 = bf16[1024,256]{1,0:T(8,128)(2,1)S(1)} copy-done((bf16[1024,256]{1,0:T(8,128)(2,1)S(1)}, bf16[1024,256]{1,0:T(8,128)(2,1)}, u32[]{:S(2)}) %copy-start.3) | copy-done | bytes 524312
  4.8 0.0 copy-start.4
  4.8 0.7 copy-done.4
  5.5 0.0 copy-start.5
  5.5 0.7 copy-done.5
  6.2 77.3 %hyena.1 = (bf16[1024,256]{1,0:T(8,128)(2,1)S(1)}, f32[512,1024]{1,0:T(8,128)S(1)}) custom-call(bf16[1024,256]{1,0:T(8,128)(2,1)S(1)} %copy-done, f32[1024]{0:T(1024)S(1)} %copy-done.4, f32[1024,128]{1,0:T(8,128)S(1)} %copy-done.1, bf16[1024,256]{1,0:T(8,128)(2,1)S(1)} %copy-done.2, f32[1024]{0:T(1024)S(1)} %copy-done.5, bf16[1024,256]{1,0:T(8,128)(2,1)S(1)} %copy-done.3, ...), custom_call_target="tpu_custom_call" | custom-call | tf_op jit(solution)/shard_map/hyena/pallas_call | solution.py:399
  83.5 0.8 copy.11
  84.3 1.3 %copy.12 = f32[512,1024]{1,0:T(8,128)} copy(f32[512,1024]{1,0:T(8,128)S(1)} %get-tuple-element.5) | data formatting | bytes 4194304
Async XLA Ops:
  0.6 1.0 %copy-start = (bf16[1024,256]{1,0:T(8,128)(2,1)S(1)}, bf16[1024,256]{1,0:T(8,128)(2,1)}, u32[]{:S(2)}) copy-start(bf16[1024,256]{1,0:T(8,128)(2,1)} %hidden.1) | copy-start | bytes 1572868
  1.7 1.0 %copy-start.1 = (f32[1024,128]{1,0:T(8,128)S(1)}, f32[1024,128]{1,0:T(8,128)}, u32[]{:S(2)}) copy-start(f32[1024,128]{1,0:T(8,128)} %taps.1) | copy-start | bytes 1572868
  2.7 1.0 %copy-start.2 = (bf16[1024,256]{1,0:T(8,128)(2,1)S(1)}, bf16[1024,256]{1,0:T(8,128)(2,1)}, u32[]{:S(2)}) copy-start(bf16[1024,256]{1,0:T(8,128)(2,1)} %filt.1) | copy-start | bytes 1572868
  3.8 1.0 %copy-start.3 = (bf16[1024,256]{1,0:T(8,128)(2,1)S(1)}, bf16[1024,256]{1,0:T(8,128)(2,1)}, u32[]{:S(2)}) copy-start(bf16[1024,256]{1,0:T(8,128)(2,1)} %gate.1) | copy-start | bytes 1572868
  4.8 0.7 copy-start.4
  5.5 0.7 copy-start.5

commit v3 on v2

--- a/solution.py
+++ b/solution.py
@@ -326,7 +326,7 @@
         copy = remote(piece(me, g), piece(me, g), mix_send.at[g, 0], mix_recv.at[g, me], other)
         copy.start()
         sends.append(copy)
-        if g == 0:
+        if g == min(1, groups - 1):
             share_part()
         if g > 0:
             forward(g - 1)

time: 86 us -> 93.7 us (1.090)
  the two profiles are of different devices: /device:TPU:0 before, /device:TPU:11 now
where the time goes in v3:
time: 93.7 us; the launch traced here: 93.4 us
  Pallas kernels  85.1 us (91%)
  local copies, waits for them, and re-layouts  7.64 us (8%)
    pallas_call x1, Pallas kernels, shards(): pl.pallas_call(functools.partial(body, n, nz, groups), out_shape=(jax.Sha...  85.1 us
    unnamed x14, local copies, waits for them, and re-layouts  7.64 us

profile of v3, /device:TPU:11, one launch (start us, length us, event | category | flops | bytes accessed | tf_op | source)
XLA Modules:
  0.0 93.4 jit_solution(4295740221180881088)
XLA Ops:
  0.6 0.0 copy-start
  0.6 1.0 %copy-done = bf16[1024,256]{1,0:T(8,128)(2,1)S(1)} copy-done((bf16[1024,256]{1,0:T(8,128)(2,1)S(1)}, bf16[1024,256]{1,0:T(8,128)(2,1)}, u32[]{:S(2)}) %copy-start) | copy-done | bytes 524312
  1.7 0.0 copy-start.1
  1.7 1.0 %copy-done.1 = f32[1024,128]{1,0:T(8,128)S(1)} copy-done((f32[1024,128]{1,0:T(8,128)S(1)}, f32[1024,128]{1,0:T(8,128)}, u32[]{:S(2)}) %copy-start.1) | copy-done | bytes 524312
  2.7 0.0 copy-start.2
  2.7 1.0 %copy-done.2 = bf16[1024,256]{1,0:T(8,128)(2,1)S(1)} copy-done((bf16[1024,256]{1,0:T(8,128)(2,1)S(1)}, bf16[1024,256]{1,0:T(8,128)(2,1)}, u32[]{:S(2)}) %copy-start.2) | copy-done | bytes 524312
  3.8 0.0 copy-start.3
  3.8 1.0 %copy-done.3 = bf16[1024,256]{1,0:T(8,128)(2,1)S(1)} copy-done((bf16[1024,256]{1,0:T(8,128)(2,1)S(1)}, bf16[1024,256]{1,0:T(8,128)(2,1)}, u32[]{:S(2)}) %copy-start.3) | copy-done | bytes 524312
  4.8 0.0 copy-start.4
  4.8 0.7 copy-done.4
  5.5 0.0 copy-start.5
  5.5 0.7 copy-done.5
  6.2 85.1 %hyena.1 = (bf16[1024,256]{1,0:T(8,128)(2,1)S(1)}, f32[512,1024]{1,0:T(8,128)S(1)}) custom-call(bf16[1024,256]{1,0:T(8,128)(2,1)S(1)} %copy-done, f32[1024]{0:T(1024)S(1)} %copy-done.4, f32[1024,128]{1,0:T(8,128)S(1)} %copy-done.1, bf16[1024,256]{1,0:T(8,128)(2,1)S(1)} %copy-done.2, f32[1024]{0:T(1024)S(1)} %copy-done.5, bf16[1024,256]{1,0:T(8,128)(2,1)S(1)} %copy-done.3, ...), custom_call_target="tpu_custom_call" | custom-call | tf_op jit(solution)/shard_map/hyena/pallas_call | solution.py:399
  91.3 0.8 copy.11
  92.0 1.3 %copy.12 = f32[512,1024]{1,0:T(8,128)} copy(f32[512,1024]{1,0:T(8,128)S(1)} %get-tuple-element.5) | data formatting | bytes 4194304
Async XLA Ops:
  0.6 1.0 %copy-start = (bf16[1024,256]{1,0:T(8,128)(2,1)S(1)}, bf16[1024,256]{1,0:T(8,128)(2,1)}, u32[]{:S(2)}) copy-start(bf16[1024,256]{1,0:T(8,128)(2,1)} %hidden.1) | copy-start | bytes 1572868
  1.7 1.0 %copy-start.1 = (f32[1024,128]{1,0:T(8,128)S(1)}, f32[1024,128]{1,0:T(8,128)}, u32[]{:S(2)}) copy-start(f32[1024,128]{1,0:T(8,128)} %taps.1) | copy-start | bytes 1572868
  2.7 1.0 %copy-start.2 = (bf16[1024,256]{1,0:T(8,128)(2,1)S(1)}, bf16[1024,256]{1,0:T(8,128)(2,1)}, u32[]{:S(2)}) copy-start(bf16[1024,256]{1,0:T(8,128)(2,1)} %filt.1) | copy-start | bytes 1572868
  3.8 1.0 %copy-start.3 = (bf16[1024,256]{1,0:T(8,128)(2,1)S(1)}, bf16[1024,256]{1,0:T(8,128)(2,1)}, u32[]{:S(2)}) copy-start(bf16[1024,256]{1,0:T(8,128)(2,1)} %gate.1) | copy-start | bytes 1572868
  4.8 0.7 copy-start.4
  5.5 0.7 copy-start.5
